TPU v7x, 32 devices: a whole 2x2x4 slice. The times are simulated.
32 devices in a mesh: ctx: 16 (over z, y, core), tp: 2 (over x).
Axes of the slice: x: 2, y: 2, z: 4, core: 2. Of those that a mesh axis runs over, the one named last changes fastest.
Arguments:
- queries: bfloat16 [1024, 1536], P('ctx', 'tp'), may hold values from -512 to 512
- keys: bfloat16 [1024, 1536], P('ctx', 'tp'), may hold values from -8 to 8
- values: bfloat16 [1024, 1536], P('ctx', 'tp'), may hold values from -6 to 6
- wo: bfloat16 [1536, 3072], P('tp'), may hold values from -0.15625 to 0.15625
- frame_tokens: int32 [16], replicated, may hold values from 32 to 64, as said below
Outputs:
- projected: bfloat16 [1024, 3072], P(('ctx', 'tp'))
Inputs may be any that keep to these rules, and one draw needn't show every extreme that they name: `frame_tokens`: at least 32 tokens of every frame are live.
All inputs are finite; a program needn't handle non-finite values.
Results may differ from a plain program's by a relative error of at most 0.014.
Values may be sent and summed in bfloat16 or wider, within the bound.
A program may use at most 128 MiB of HBM per device.

v0:
```python
import functools
import math

import jax
import jax.numpy as jnp
from jax import lax
from jax.experimental import pallas as pl
from jax.experimental.pallas import tpu as pltpu
from jax.sharding import PartitionSpec as P

HEAD_DIM = 128
LAYER = 4
NEG = -1e30
MESH = pl.DeviceIdType.MESH
KEYS, VALUES = 0, 1
UP, SIDE, CORE, CROSS, UP_SIDE = 0, 1, 2, 3, 4


def group_levels(levels):
    return levels // 2 if levels % 2 == 0 else levels


def wings_of(head_count):
    return 2 if head_count % 2 == 0 else 1


def kernel(
    n,
    chunk,
    counts_ref,
    q_hbm,
    k_hbm,
    v_hbm,
    wo_hbm,
    out_ref,
    q_ref,
    q_sem,
    k_all,
    v_all,
    wo_all,
    run_max,
    run_acc,
    guest_q,
    guest_max,
    guest_sum,
    guest_acc,
    guest_stats,
    far_acc,
    far_stats,
    attended,
    kept,
    outgoing,
    incoming,
    send_sem,
    recv_sem,
    local_sem,
    wo_sem,
    x_send_sem,
    x_recv_sem,
    q_send_sem,
    q_recv_sem,
    back_send_sem,
    back_recv_sem,
):
    tok_rows, columns = q_hbm.shape
    wings = wings_of(columns // HEAD_DIM)
    breadth = columns // wings
    last_wing = wings - 1
    head_count = columns // HEAD_DIM
    width = wo_hbm.shape[1]
    half = tok_rows // 2
    me = lax.axis_index("ctx")
    tp = lax.axis_index("tp")
    levels = n // LAYER
    group = group_levels(levels)
    guests = levels - group
    level = me // LAYER
    is_upper = level >= group
    local = lax.rem(level, group)
    is_host = level == (group - 1 if guests else levels)
    lane = lax.rem(me, LAYER)
    base = level * LAYER
    side_y = lax.rem(lane + 2, LAYER)
    core_lane = lane + 1 - 2 * lax.rem(lane, 2)
    cross_lane = lax.rem(core_lane + 2, LAYER)
    above = lax.rem(me + LAYER, n)
    below = lax.rem(me + n - LAYER, n)
    has_above = local < group - 1
    has_below = local > 0
    host = (group - 1) * LAYER + lane
    guest_slot = lax.rem(level, group)
    side_dev, core_dev = base + side_y, base + core_lane
    halls = (k_all, v_all)
    inputs = (k_hbm, v_hbm)

    wo_copy = pltpu.make_async_copy(wo_hbm, wo_all, wo_sem)
    wo_copy.start()

    def rows_of(src):
        return pl.ds(pl.multiple_of(src * tok_rows, tok_rows), tok_rows)

    q_copy = pltpu.make_async_copy(q_hbm, q_ref, q_sem)
    q_copy.start()

    def wing_cols(w):
        return slice(w * breadth, (w + 1) * breadth)

    own = [
        pltpu.make_async_copy(inputs[p], halls[p].at[rows_of(me)], local_sem.at[p])
        for p in range(2)
    ]
    for p in range(2):
        own[p].start()

    barrier = pltpu.get_barrier_semaphore()

    def greet(dev, other_tp):
        pl.semaphore_signal(barrier, inc=1, device_id=(dev, other_tp), device_id_type=MESH)

    @pl.when(has_above)
    def _():
        greet(above, tp)

    @pl.when(has_below)
    def _():
        greet(below, tp)

    greet(side_dev, tp)
    greet(core_dev, tp)
    greet(me, 1 - tp)

    @pl.when(is_upper)
    def _():
        greet(host, tp)

    @pl.when(is_host)
    def _():
        def greet_guest(j, carry):
            greet(me + LAYER * (1 + j), tp)
            return carry

        lax.fori_loop(0, guests, greet_guest, 0)

    pl.semaphore_wait(
        barrier,
        3
        + has_above.astype(jnp.int32)
        + has_below.astype(jnp.int32)
        + is_upper.astype(jnp.int32)
        + guests * is_host.astype(jnp.int32),
    )

    def ask(j, w):
        return pltpu.make_async_remote_copy(
            src_ref=q_ref.at[:, wing_cols(w)],
            dst_ref=guest_q.at[rows_of(j), wing_cols(w)],
            send_sem=q_send_sem.at[w],
            recv_sem=q_recv_sem.at[w, j],
            device_id=(host, tp),
            device_id_type=MESH,
        )

    def answer(j, p, w):
        source, target = (
            (guest_acc.at[j, :, wing_cols(w)], far_acc.at[:, wing_cols(w)]),
            (guest_stats.at[j, w], far_stats.at[w]),
        )[p]
        return pltpu.make_async_remote_copy(
            src_ref=source,
            dst_ref=target,
            send_sem=back_send_sem.at[p, w, j],
            recv_sem=back_recv_sem.at[p, w],
            device_id=(lax.rem(me + LAYER * (1 + j), n), tp),
            device_id_type=MESH,
        )

    q_copy.wait()
    if guests:

        @pl.when(is_upper)
        def _():
            for w in range(wings):
                ask(guest_slot, w).start()

    def piece(p, w, kind, step, src, dev):
        where = halls[p].at[rows_of(src), wing_cols(w)]
        return pltpu.make_async_remote_copy(
            src_ref=where,
            dst_ref=where,
            send_sem=send_sem.at[kind, p * wings + w, step],
            recv_sem=recv_sem.at[p * wings + w, src],
            device_id=(dev, tp),
            device_id_type=MESH,
        )

    def rise_own(p, w):
        @pl.when(has_above)
        def _():
            piece(p, w, UP, 0, me, above).start()

    def forward_chain(p, w, step):
        src = me - LAYER * step
        piece(p, w, UP, step, src, above).wait_recv()

        @pl.when(has_above)
        def _():
            piece(p, w, UP, step, src, above).start()

        if p == VALUES:
            piece(p, w, SIDE, step, src, side_dev).start()
        piece(p, w, CORE, step, src, core_dev).start()

    def forward_side(p, w, step):
        src = base + side_y - LAYER * step
        piece(p, w, CROSS, step, src, core_dev).wait_recv()
        if p == KEYS:

            @pl.when(has_above)
            def _():
                piece(p, w, UP_SIDE, step, src, above).start()

        piece(p, w, CROSS, step, src, core_dev).start()

    def wait_core(w, step):
        for p in range(2):
            for other in (core_lane, cross_lane):
                piece(p, w, CORE, step, base + other - LAYER * step, core_dev).wait_recv()

    span = LAYER * tok_rows
    col = lax.broadcasted_iota(jnp.int32, (1, span), 1)
    slot = col // tok_rows
    place = lax.rem(col, tok_rows)
    scale = math.log2(math.e) / math.sqrt(HEAD_DIM)
    ones = jnp.ones((span, HEAD_DIM), jnp.bfloat16)
    head_cols = [slice(h * HEAD_DIM, (h + 1) * HEAD_DIM) for h in range(head_count)]

    each = head_count // wings
    wing_heads = [range(w * each, (w + 1) * each) for w in range(wings)]

    def attend(step, query, max_ref, acc_ref, rows, causal, w):
        heads = wing_heads[w]
        cols_of = [head_cols[h] for h in heads]
        first = base - LAYER * step
        limit = jnp.zeros((1, span), jnp.int32)
        for f in range(LAYER):
            live = counts_ref[first + f]
            if causal:
                live = jnp.where(first + f <= me, live, 0)
            limit = jnp.where(slot == f, live, limit)
        allowed = place < limit
        keys_at = pl.ds(pl.multiple_of(first * tok_rows, span), span)
        scores = [
            lax.dot_general(
                query(cols),
                k_all[keys_at, cols],
                (((1,), (1,)), ((), ())),
                preferred_element_type=jnp.float32,
            )
            for cols in cols_of
        ]
        scores = [jnp.where(allowed, one, NEG) for one in scores]
        old_max = [max_ref[h, rows, :][:, :1] for h in heads]
        new_max = [
            jnp.maximum(old, jnp.max(one, axis=-1, keepdims=True))
            for old, one in zip(old_max, scores)
        ]
        weights = [
            jnp.exp2((one - top) * scale).astype(jnp.bfloat16)
            for one, top in zip(scores, new_max)
        ]
        added = [
            jnp.dot(
                one,
                jnp.concatenate([v_all[keys_at, cols], ones], axis=1),
                preferred_element_type=jnp.float32,
            )
            for one, cols in zip(weights, cols_of)
        ]
        for i, h in enumerate(heads):
            fade = jnp.exp2((old_max[i] - new_max[i]) * scale)
            max_ref[h, rows, :] = jnp.broadcast_to(new_max[i], (fade.shape[0], HEAD_DIM))
            acc_ref[h, rows, :] = fade * acc_ref[h, rows, :] + added[i]

    def attend_own(step, w):
        attend(step, lambda cols: q_ref[:, cols], run_max, run_acc, slice(0, tok_rows), True, w)

    def turn(block):
        missing = jnp.zeros((HEAD_DIM - block.shape[0], HEAD_DIM), jnp.float32)
        return jnp.transpose(jnp.concatenate([block, missing], axis=0))

    spot = lax.broadcasted_iota(jnp.int32, (tok_rows, HEAD_DIM), 1)
    pack = 2 if guests % 2 == 0 else 1

    def attend_guests(step, last, w):
        if not guests:
            return

        @pl.when(is_host)
        def _():
            def one(i, carry):
                block = guests // pack - 1 - i

                @pl.when(step == 0)
                def _():
                    for g in range(pack):
                        ask(block * pack + g, w).wait_recv()

                rows = pl.ds(pl.multiple_of(block * pack * tok_rows, tok_rows), pack * tok_rows)
                attend(
                    step, lambda cols: guest_q[rows, cols], guest_max, guest_sum, rows, False, w
                )
                if last:
                    for g in reversed(range(pack)):
                        j = block * pack + g
                        at = rows_of(j)
                        stats = jnp.zeros((tok_rows, HEAD_DIM), jnp.float32)
                        for i, h in enumerate(wing_heads[w]):
                            stats = jnp.where(spot == i, guest_max[h, at, :], stats)
                            stats = jnp.where(
                                spot == each + i, guest_sum[h, at, HEAD_DIM:], stats
                            )
                            guest_acc[j, :, head_cols[h]] = guest_sum[h, at, :HEAD_DIM].astype(
                                jnp.bfloat16
                            )
                        guest_stats[j, w] = turn(stats)[: guest_stats.shape[2]]
                        answer(j, 0, w).start()
                        answer(j, 1, w).start()
                return carry

            lax.fori_loop(0, guests // pack, one, 0)

    run_max[...] = jnp.full(run_max.shape, NEG, jnp.float32)
    run_acc[...] = jnp.zeros(run_acc.shape, jnp.float32)

    @pl.when(is_host)
    def _():
        guest_max[...] = jnp.full(guest_max.shape, NEG, jnp.float32)
        guest_sum[...] = jnp.zeros(guest_sum.shape, jnp.float32)

    for p in (VALUES, KEYS):
        own[p].wait()
    rise_own(VALUES, 0)
    rise_own(KEYS, 0)
    for p in (KEYS, VALUES):
        piece(p, 0, SIDE, 0, me, side_dev).start()
        piece(p, 0, CORE, 0, me, core_dev).start()
    if last_wing:
        rise_own(VALUES, 1)
        piece(KEYS, 1, SIDE, 0, me, side_dev).start()
        for p in (KEYS, VALUES):
            piece(p, 1, CORE, 0, me, core_dev).start()
    forward_side(KEYS, 0, 0)
    if last_wing:
        rise_own(KEYS, 1)

    @pl.when(has_below)
    def _():
        forward_chain(VALUES, 0, 1)

    if last_wing:
        piece(VALUES, 1, SIDE, 0, me, side_dev).start()

    def body(step, carry):
        forward_side(VALUES, 0, step - 1)
        forward_chain(KEYS, 0, step)
        if last_wing:
            forward_side(KEYS, 1, step - 1)
            forward_chain(VALUES, 1, step)
        forward_side(KEYS, 0, step)
        if last_wing:
            forward_chain(KEYS, 1, step)
            forward_side(VALUES, 1, step - 1)

        @pl.when(step < local)
        def _():
            forward_chain(VALUES, 0, step + 1)

        return carry

    lax.fori_loop(1, local + 1, body, 0)

    for w in range(wings):
        forward_side(VALUES, w, local)
        if w:
            forward_side(KEYS, w, local)

        def early(step, carry):
            wait_core(w, step)
            attend_guests(step, False, w)
            return carry

        lax.fori_loop(0, local, early, 0)
        wait_core(w, local)
        attend_guests(local, True, w)

    for w in range(wings):

        def own_step(step, carry):
            attend_own(step, w)
            return carry

        lax.fori_loop(0, local + 1, own_step, 0)

    if guests:

        @pl.when(is_upper)
        def _():
            for w in range(wings):
                answer(0, 0, w).wait_recv()
                answer(0, 1, w).wait_recv()
                stats = turn(far_stats[w])[:tok_rows]
                for i, h in enumerate(wing_heads[w]):
                    far_max = stats[:, i : i + 1]
                    far_total = stats[:, each + i : each + i + 1]
                    old_max = run_max[h][:, :1]
                    new_max = jnp.maximum(old_max, far_max)
                    fade = jnp.exp2((old_max - new_max) * scale)
                    far_fade = jnp.exp2((far_max - new_max) * scale)
                    far = jnp.concatenate(
                        [
                            far_acc[:, head_cols[h]].astype(jnp.float32),
                            jnp.broadcast_to(far_total, (tok_rows, HEAD_DIM)),
                        ],
                        axis=1,
                    )
                    run_acc[h] = fade * run_acc[h] + far_fade * far

    row = lax.broadcasted_iota(jnp.int32, (tok_rows, HEAD_DIM), 0)
    row_live = row < counts_ref[me]
    for h in range(head_count):
        out = jnp.where(row_live, run_acc[h, :, :HEAD_DIM] / run_acc[h, :, HEAD_DIM:], 0.0)
        attended[:, head_cols[h]] = out.astype(jnp.bfloat16)

    wo_copy.wait()
    theirs = attended[pl.ds(pl.multiple_of((1 - tp) * half, half), half), :]
    mine = attended[pl.ds(pl.multiple_of(tp * half, half), half), :]
    lhs = jnp.concatenate([theirs, mine], axis=0)

    def swap(c):
        return pltpu.make_async_remote_copy(
            src_ref=outgoing.at[c],
            dst_ref=incoming.at[c],
            send_sem=x_send_sem.at[c],
            recv_sem=x_recv_sem.at[c],
            device_id=(me, 1 - tp),
            device_id_type=MESH,
        )

    for c in range(width // chunk):
        part = jnp.dot(
            lhs, wo_all[:, c * chunk : (c + 1) * chunk], preferred_element_type=jnp.float32
        )
        outgoing[c] = part[:half].astype(jnp.bfloat16)
        swap(c).start()
        kept[c] = part[half:]

    def drain(step, carry):
        for w in range(wings):
            for p in (KEYS, VALUES):

                @pl.when(has_above)
                def _():
                    piece(p, w, UP, step, me, above).wait_send()
                    if p == KEYS:
                        piece(p, w, UP_SIDE, step, me, above).wait_send()

                if p == VALUES:
                    piece(p, w, SIDE, step, me, side_dev).wait_send()
                piece(p, w, CORE, step, me, core_dev).wait_send()
                piece(p, w, CROSS, step, me, core_dev).wait_send()
        return carry

    for w in range(wings):
        piece(KEYS, w, SIDE, 0, me, side_dev).wait_send()
    lax.fori_loop(0, local + 1, drain, 0)
    if guests:

        @pl.when(is_upper)
        def _():
            for w in range(wings):
                ask(guest_slot, w).wait_send()

        @pl.when(is_host)
        def _():
            def drain_guest(j, carry):
                for w in range(wings):
                    answer(j, 0, w).wait_send()
                    answer(j, 1, w).wait_send()
                return carry

            lax.fori_loop(0, guests, drain_guest, 0)

    for c in range(width // chunk):
        swap(c).wait_recv()
        out_ref[:, c * chunk : (c + 1) * chunk] = (
            kept[c] + incoming[c].astype(jnp.float32)
        ).astype(out_ref.dtype)
    for c in range(width // chunk):
        swap(c).wait_send()


def on_device(queries, keys, values, wo, frame_tokens):
    tok_rows, columns = queries.shape
    width = wo.shape[1]
    n = lax.axis_size("ctx")
    half = tok_rows // 2
    chunk = 512 if width % 512 == 0 else width
    chunks = width // chunk
    head_count = columns // HEAD_DIM
    levels = n // LAYER
    guests = levels - group_levels(levels)
    room = max(guests, 1)
    wings = wings_of(head_count)
    stat_rows = -(-2 * head_count // wings // 8) * 8
    vmem = pltpu.VMEM
    dma = pltpu.SemaphoreType.DMA
    return pl.pallas_call(
        functools.partial(kernel, n, chunk),
        out_shape=jax.ShapeDtypeStruct((half, width), jnp.bfloat16),
        in_specs=[
            pl.BlockSpec(memory_space=pltpu.SMEM),
            pl.BlockSpec(memory_space=pltpu.HBM),
            pl.BlockSpec(memory_space=pltpu.HBM),
            pl.BlockSpec(memory_space=pltpu.HBM),
            pl.BlockSpec(memory_space=pltpu.HBM),
        ],
        out_specs=pl.BlockSpec(memory_space=vmem),
        scratch_shapes=[
            vmem((tok_rows, columns), jnp.bfloat16),
            dma,
            vmem((n * tok_rows, columns), jnp.bfloat16),
            vmem((n * tok_rows, columns), jnp.bfloat16),
            vmem(wo.shape, jnp.bfloat16),
            vmem((head_count, tok_rows, HEAD_DIM), jnp.float32),
            vmem((head_count, tok_rows, 2 * HEAD_DIM), jnp.float32),
            vmem((room * tok_rows, columns), jnp.bfloat16),
            vmem((head_count, room * tok_rows, HEAD_DIM), jnp.float32),
            vmem((head_count, room * tok_rows, 2 * HEAD_DIM), jnp.float32),
            vmem((room, tok_rows, columns), jnp.bfloat16),
            vmem((room, wings, stat_rows, HEAD_DIM), jnp.float32),
            vmem((tok_rows, columns), jnp.bfloat16),
            vmem((wings, stat_rows, HEAD_DIM), jnp.float32),
            vmem((tok_rows, columns), jnp.bfloat16),
            vmem((chunks, half, chunk), jnp.float32),
            vmem((chunks, half, chunk), jnp.bfloat16),
            vmem((chunks, half, chunk), jnp.bfloat16),
            dma((5, 2 * wings, levels)),
            dma((2 * wings, n)),
            dma((2,)),
            dma,
            dma((chunks,)),
            dma((chunks,)),
            dma((wings,)),
            dma((wings, room)),
            dma((2, wings, room)),
            dma((2, wings)),
        ],
        compiler_params=pltpu.CompilerParams(
            collective_id=0, has_side_effects=True, vmem_limit_bytes=52 << 20
        ),
    )(*[pltpu.with_memory_space_constraint(x, pltpu.HBM) for x in (frame_tokens, queries, keys, values, wo)])


def solution(mesh):
    in_specs = (P("ctx", "tp"), P("ctx", "tp"), P("ctx", "tp"), P("tp", None), P())
    out_specs = P(("ctx", "tp"), None)
    return jax.shard_map(
        on_device, mesh=mesh, in_specs=in_specs, out_specs=out_specs, check_vma=False
    )
```

profile of v0, /device:TPU:16, one launch (start us, length us, event | category | flops | bytes accessed | tf_op | source)
XLA Modules:
  0.0 28.5 jit_solution(15081514477486144690)
XLA Ops:
  0.0 27.8 %shard_map.55 = bf16[32,3072]{1,0:T(8,128)(2,1)S(1)} custom-call(s32[16]{0:T(128)} %counts_ref.1, bf16[64,768]{1,0:T(8,128)(2,1)} %q_hbm.1, bf16[64,768]{1,0:T(8,128)(2,1)} %k_hbm.1, bf16[64,768]{1,0:T(8,128)(2,1)} %v_hbm.1, bf16[768,3072]{1,0:T(8,128)(2,1)} %wo_hbm.1), custom_call_target="tpu_custom_call" | custom-call | tf_op jit(solution)/shard_map/pallas_call | solution.py:517
  27.8 0.7 %copy.7 = bf16[32,3072]{1,0:T(8,128)(2,1)} copy(bf16[32,3072]{1,0:T(8,128)(2,1)S(1)} %shard_map.55) | data formatting | bytes 393216
where the time goes:
time: 28.6 us; the launch traced here: 28.5 us
  Pallas kernels  27.8 us (97%)
  local copies, waits for them, and re-layouts  0.68 us (2%)
    pallas_call x1, Pallas kernels, on_device(): pl.pallas_call(functools.partial(kernel, n, chunk), out_shape=jax.ShapeDt...  27.8 us
    unnamed x1, local copies, waits for them, and re-layouts  0.68 us

commit v1 on v0

v1 whole, which is shorter than its diff:
```python
import functools
import math

import jax
import jax.numpy as jnp
from jax import lax
from jax.experimental import pallas as pl
from jax.experimental.pallas import tpu as pltpu
from jax.sharding import PartitionSpec as P

HEAD_DIM = 128
LAYER = 4
BLOCKS = 2
NEG = -1e30
MESH = pl.DeviceIdType.MESH
FAR, NEAR = 0, 1


def group_size(n):
    levels = n // LAYER
    return n // 2 if levels % 2 == 0 else n


def host_offsets(size, head_count):
    top = size // LAYER - 1
    places = []
    for h in range(head_count):
        spread = h % LAYER
        places.append((top - h // LAYER) * LAYER + (spread % 2) * (LAYER // 2) + spread // 2)
    return places


def kernel(
    n,
    chunk,
    counts_ref,
    q_hbm,
    k_hbm,
    v_hbm,
    wo_hbm,
    out_ref,
    q_ref,
    k_ref,
    v_ref,
    wo_all,
    k_in,
    v_in,
    q_in,
    acc_out,
    stat_out,
    acc_in,
    stat_in,
    stat_rows,
    attended,
    kept,
    outgoing,
    incoming,
    in_sem,
    wo_sem,
    k_send,
    v_send,
    q_send,
    far_send,
    k_recv,
    v_recv,
    q_recv,
    far_recv,
    acc_send,
    acc_recv,
    stat_send,
    stat_recv,
    x_send_sem,
    x_recv_sem,
):
    tok_rows, columns = k_hbm.shape
    head_count = columns // HEAD_DIM
    width = wo_hbm.shape[1]
    half = tok_rows // 2
    blocks = q_ref.shape[0]
    rb = q_ref.shape[1]
    sent_blocks = blocks // 2
    me = lax.axis_index("ctx")
    tp = lax.axis_index("tp")
    size = group_size(n)
    split = size < n
    upper = me // size
    base = upper * size
    local = me - base
    is_upper = upper > 0
    places = host_offsets(size, head_count)
    my_head = jnp.int32(0)
    is_host = local < 0
    for h, place in enumerate(places):
        my_head = jnp.where(local == place, h, my_head)
        is_host = jnp.logical_or(is_host, local == place)
    my_cols = pl.ds(pl.multiple_of(my_head * HEAD_DIM, HEAD_DIM), HEAD_DIM)
    head_cols = [slice(h * HEAD_DIM, (h + 1) * HEAD_DIM) for h in range(head_count)]
    scale = math.log2(math.e) / math.sqrt(HEAD_DIM)

    def start_of(b):
        side = (1 - tp) if b < sent_blocks else tp
        return pl.multiple_of(side * half + (b % sent_blocks) * rb, rb)

    def rows_of(src, rows):
        return pl.ds(pl.multiple_of(src * rows, rows), rows)

    loads = [
        pltpu.make_async_copy(k_hbm, k_ref, in_sem.at[0]),
        pltpu.make_async_copy(v_hbm, v_ref, in_sem.at[1]),
    ] + [
        pltpu.make_async_copy(q_hbm.at[pl.ds(start_of(b), rb), :], q_ref.at[b], in_sem.at[2 + b])
        for b in range(blocks)
    ]
    for load in loads:
        load.start()

    barrier = pltpu.get_barrier_semaphore()

    def greet(dev, other_tp):
        pl.semaphore_signal(barrier, inc=1, device_id=(dev, other_tp), device_id_type=MESH)

    def each(count, body):
        if count <= 16:
            for j in range(count):
                body(j)
        else:
            lax.fori_loop(0, count, lambda j, carry: (body(j), carry)[1], 0)

    greet(me, 1 - tp)

    @pl.when(is_host)
    def _():
        def other(j):
            @pl.when(local != j)
            def _():
                greet(base + j, tp)

        each(size, other)

    @pl.when(jnp.logical_not(is_host))
    def _():
        for place in places:
            greet(base + place, tp)

    expected = 1 + jnp.where(is_host, size - 1, head_count)
    if split:

        @pl.when(is_upper)
        def _():
            for place in places:
                greet(place, tp)

        @pl.when(jnp.logical_and(is_host, jnp.logical_not(is_upper)))
        def _():
            each(size, lambda j: greet(size + j, tp))

        expected = expected + jnp.where(is_upper, head_count, jnp.where(is_host, size, 0))
    with jax.named_scope("bar"):
        pl.semaphore_wait(barrier, expected)

    wo_copy = pltpu.make_async_copy(wo_hbm, wo_all, wo_sem)

    def remote(src, dst, send, recv, dev):
        return pltpu.make_async_remote_copy(
            src_ref=src,
            dst_ref=dst,
            send_sem=send,
            recv_sem=recv,
            device_id=(dev, tp),
            device_id_type=MESH,
        )

    def give_k(h, frame, dev):
        return remote(
            k_ref.at[:, head_cols[h]], k_in.at[rows_of(frame, tok_rows)], k_send.at[h], k_recv.at[frame], dev
        )

    def give_v(h, frame, dev):
        return remote(
            v_ref.at[:, head_cols[h]], v_in.at[rows_of(frame, tok_rows)], v_send.at[h], v_recv.at[frame], dev
        )

    def give_q(h, frame, dev):
        return remote(
            q_ref.at[:, :, head_cols[h]], q_in.at[NEAR, :, rows_of(frame, rb)], q_send.at[h], q_recv.at[frame], dev
        )

    def give_far(h, b, frame):
        return remote(
            q_ref.at[b, :, head_cols[h]],
            q_in.at[FAR, b, rows_of(frame, rb)],
            far_send.at[b, h],
            far_recv.at[b, frame],
            places[h],
        )

    def own_copies():
        return (
            pltpu.make_async_copy(k_ref.at[:, my_cols], k_in.at[rows_of(local, tok_rows)], k_recv.at[local]),
            pltpu.make_async_copy(v_ref.at[:, my_cols], v_in.at[rows_of(local, tok_rows)], v_recv.at[local]),
            pltpu.make_async_copy(
                q_ref.at[:, :, my_cols], q_in.at[NEAR, :, rows_of(local, rb)], q_recv.at[local]
            ),
        )

    with jax.named_scope("own"):
        for load in loads:
            load.wait()

    def to_hosts(give):
        for h, place in enumerate(places):

            @pl.when(local != place)
            def _():
                give(h, local, base + place).start()

    if split:

        @pl.when(is_upper)
        def _():
            for b in range(sent_blocks):
                for h in range(head_count):
                    give_far(h, b, local).start()

    to_hosts(give_k)
    to_hosts(give_v)
    to_hosts(give_q)

    @pl.when(is_host)
    def _():
        for copy in own_copies():
            copy.start()

    if split:

        @pl.when(is_upper)
        def _():
            for b in range(sent_blocks, blocks):
                for h in range(head_count):
                    give_far(h, b, local).start()

    wo_copy.start()

    tile_frames = min(size, 256 // rb)
    tile_rows = tile_frames * rb
    slab_frames = HEAD_DIM // rb
    slabs = tile_rows // HEAD_DIM
    span_frames = min(size, 8)
    span = span_frames * tok_rows
    key_tiles = size // span_frames
    col = lax.broadcasted_iota(jnp.int32, (1, span), 1)
    slot = col // tok_rows
    place_in = lax.rem(col, tok_rows)
    tile_row = lax.broadcasted_iota(jnp.int32, (tile_rows, 1), 0)
    ones = jnp.ones((span, HEAD_DIM), jnp.bfloat16)
    lane = lax.broadcasted_iota(jnp.int32, (tile_rows, HEAD_DIM), 1)

    def live_keys(kt):
        limit = jnp.zeros((1, span), jnp.int32)
        for f in range(span_frames):
            limit = jnp.where(slot == f, counts_ref[base + kt * span_frames + f], limit)
        return place_in < limit

    def attend(query, kind, first_frame):
        def part(kt, old_max):
            keys_at = rows_of(kt, span) if key_tiles > 1 else slice(0, span)
            scores = lax.dot_general(
                query, k_in[keys_at, :], (((1,), (1,)), ((), ())), preferred_element_type=jnp.float32
            )
            allowed = live_keys(kt)
            if kind == NEAR:
                allowed = jnp.logical_and(
                    allowed, slot + kt * span_frames <= first_frame + tile_row // rb
                )
            scores = jnp.where(allowed, scores, NEG)
            top = jnp.max(scores, axis=-1, keepdims=True)
            if old_max is not None:
                top = jnp.maximum(top, old_max)
            weights = jnp.exp2((scores - top) * scale).astype(jnp.bfloat16)
            added = jnp.dot(
                weights,
                jnp.concatenate([v_in[keys_at, :], ones], axis=1),
                preferred_element_type=jnp.float32,
            )
            return top, added

        top, acc = part(0, None)
        if key_tiles > 1:

            def more(kt, carry):
                old_max, acc = carry
                top, added = part(kt, old_max)
                return top, jnp.exp2((old_max - top) * scale) * acc + added

            top, acc = lax.fori_loop(1, key_tiles, more, (top, acc))
        return top, acc

    def answer(kind, b, j, dev):
        return (
            remote(
                acc_out.at[kind, b, rows_of(j, rb)],
                acc_in.at[kind, b, :, my_cols],
                acc_send.at[kind, b, j],
                acc_recv.at[kind, b, my_head],
                dev,
            ),
            remote(
                stat_out.at[kind, b, j // slab_frames],
                stat_in.at[kind, b, my_head],
                stat_send.at[kind, b, j],
                stat_recv.at[kind, b, my_head],
                dev,
            ),
        )

    def keep_answer(kind, b):
        return (
            pltpu.make_async_copy(
                acc_out.at[kind, b, rows_of(local, rb)],
                acc_in.at[kind, b, :, my_cols],
                acc_recv.at[kind, b, my_head],
            ),
            pltpu.make_async_copy(
                stat_out.at[kind, b, local // slab_frames],
                stat_in.at[kind, b, my_head],
                stat_recv.at[kind, b, my_head],
            ),
        )

    def serve(kind, b):
        for t in range(size // tile_frames):
            at = slice(t * tile_rows, (t + 1) * tile_rows)
            top, acc = attend(q_in[kind, b, at, :], kind, t * tile_frames)
            acc_out[kind, b, at, :] = acc[:, :HEAD_DIM].astype(jnp.bfloat16)
            stats = jnp.where(lane == 0, top, acc[:, HEAD_DIM:])
            for s in range(slabs):
                turned = jnp.transpose(stats[s * HEAD_DIM : (s + 1) * HEAD_DIM])
                stat_out[kind, b, t * slabs + s] = turned[:2]

            def send(i):
                j = t * tile_frames + i
                if kind == NEAR:

                    @pl.when(local != j)
                    def _():
                        for copy in answer(kind, b, j, base + j):
                            copy.start()

                    @pl.when(local == j)
                    def _():
                        for copy in keep_answer(kind, b):
                            copy.start()

                else:
                    for copy in answer(kind, b, j, size + j):
                        copy.start()

            each(tile_frames, send)

    @pl.when(is_host)
    def _():
        with jax.named_scope("wk"):
            each(size, lambda j: give_k(0, j, me).wait_recv())
        with jax.named_scope("wv"):
            each(size, lambda j: give_v(0, j, me).wait_recv())
        if split:

            @pl.when(jnp.logical_not(is_upper))
            def _():
                for b in range(blocks):
                    with jax.named_scope("wf"):
                        each(size, lambda j: give_far(0, b, j).wait_recv())
                    with jax.named_scope("sf"):
                        serve(FAR, b)

        with jax.named_scope("wq"):
            each(size, lambda j: give_q(0, j, me).wait_recv())
        for b in range(blocks):
            with jax.named_scope("sn"):
                serve(NEAR, b)

    row = lax.broadcasted_iota(jnp.int32, (rb, HEAD_DIM), 0)
    padding = jnp.zeros((HEAD_DIM - 2 * stat_rows.shape[2], HEAD_DIM), jnp.float32)

    def wait_answers(kind, b):
        for h in range(head_count):
            remote(
                acc_out.at[kind, b, rows_of(0, rb)],
                acc_in.at[kind, b, :, head_cols[h]],
                acc_send.at[kind, b, 0],
                acc_recv.at[kind, b, h],
                me,
            ).wait_recv()
            remote(
                stat_out.at[kind, b, 0],
                stat_in.at[kind, b, h],
                stat_send.at[kind, b, 0],
                stat_recv.at[kind, b, h],
                me,
            ).wait_recv()

    def stats_of(kind, b):
        for h in range(head_count):
            stat_rows[kind, 0, h : h + 1, :] = stat_in[kind, b, h, 0:1, :]
            stat_rows[kind, 1, h : h + 1, :] = stat_in[kind, b, h, 1:2, :]
        return stat_rows[kind, 0], stat_rows[kind, 1]

    def finish(kinds, factors, b):
        turned = jnp.transpose(jnp.concatenate(list(factors) + [padding] + ([padding[: factors[0].shape[0]]] if len(factors) == 1 else []), axis=0))
        stat_rows_t = attended_turn(turned)
        live = row + start_of(b) < counts_ref[me]
        for h in range(head_count):
            out = 0.0
            for i, kind in enumerate(kinds):
                at = i * factors[0].shape[0] + h
                out = out + stat_rows_t[:, at : at + 1] * acc_in[kind, b, :, head_cols[h]].astype(jnp.float32)
            attended[b, :, head_cols[h]] = jnp.where(live, out, 0.0).astype(jnp.bfloat16)

    def attended_turn(turned):
        at = lax.rem(local, slab_frames) * rb
        picked = turned[:rb]
        for i in range(1, slab_frames):
            picked = jnp.where(at == i * rb, turned[i * rb : (i + 1) * rb], picked)
        return picked

    def swap(b, c):
        return pltpu.make_async_remote_copy(
            src_ref=outgoing.at[b, c],
            dst_ref=incoming.at[b, c],
            send_sem=x_send_sem.at[b, c],
            recv_sem=x_recv_sem.at[b, c],
            device_id=(me, 1 - tp),
            device_id_type=MESH,
        )

    for b in range(blocks):
        with jax.named_scope("wan"):
            wait_answers(NEAR, b)

        def near_only():
            near_max, near_sum = stats_of(NEAR, b)
            finish((NEAR,), (1.0 / near_sum,), b)

        if split:

            @pl.when(is_upper)
            def _():
                with jax.named_scope("waf"):
                    wait_answers(FAR, b)
                near_max, near_sum = stats_of(NEAR, b)
                far_max, far_sum = stats_of(FAR, b)
                top = jnp.maximum(near_max, far_max)
                near = jnp.exp2((near_max - top) * scale)
                far = jnp.exp2((far_max - top) * scale)
                total = near * near_sum + far * far_sum
                finish((NEAR, FAR), (near / total, far / total), b)

            @pl.when(jnp.logical_not(is_upper))
            def _():
                near_only()

        else:
            near_only()

        if b == 0:
            wo_copy.wait()
        with jax.named_scope("proj"):
            lhs = attended[b]
            for c in range(width // chunk):
                part = jnp.dot(
                    lhs, wo_all[:, c * chunk : (c + 1) * chunk], preferred_element_type=jnp.float32
                )
                if b < sent_blocks:
                    outgoing[b, c] = part.astype(jnp.bfloat16)
                    swap(b, c).start()
                else:
                    kept[b - sent_blocks, c] = part

    with jax.named_scope("drain"):
        for h, place in enumerate(places):

            @pl.when(local != place)
            def _():
                give_k(h, local, base + place).wait_send()
                give_v(h, local, base + place).wait_send()
                give_q(h, local, base + place).wait_send()

        if split:

            @pl.when(is_upper)
            def _():
                for b in range(blocks):
                    for h in range(head_count):
                        give_far(h, b, local).wait_send()

            @pl.when(jnp.logical_and(is_host, jnp.logical_not(is_upper)))
            def _():
                for b in range(blocks):

                    def drain_far(j):
                        for copy in answer(FAR, b, j, size + j):
                            copy.wait_send()

                    each(size, drain_far)

        @pl.when(is_host)
        def _():
            for b in range(blocks):

                def drain_near(j):
                    @pl.when(local != j)
                    def _():
                        for copy in answer(NEAR, b, j, base + j):
                            copy.wait_send()

                each(size, drain_near)

    for b in range(sent_blocks):
        for c in range(width // chunk):
            with jax.named_scope("swapw"):
                swap(b, c).wait_recv()
            out_ref[b * rb : (b + 1) * rb, c * chunk : (c + 1) * chunk] = (
                kept[b, c] + incoming[b, c].astype(jnp.float32)
            ).astype(out_ref.dtype)
    with jax.named_scope("fin"):
        for b in range(sent_blocks):
            for c in range(width // chunk):
                swap(b, c).wait_send()


def on_device(queries, keys, values, wo, frame_tokens):
    tok_rows, columns = queries.shape
    width = wo.shape[1]
    n = lax.axis_size("ctx")
    half = tok_rows // 2
    chunk = 512 if width % 512 == 0 else width
    chunks = width // chunk
    head_count = columns // HEAD_DIM
    size = group_size(n)
    blocks = BLOCKS
    sent = blocks // 2
    rb = tok_rows // blocks
    slabs = size * rb // HEAD_DIM
    stat_pad = -(-head_count // 8) * 8
    vmem = pltpu.VMEM
    dma = pltpu.SemaphoreType.DMA
    return pl.pallas_call(
        functools.partial(kernel, n, chunk),
        out_shape=jax.ShapeDtypeStruct((half, width), jnp.bfloat16),
        in_specs=[
            pl.BlockSpec(memory_space=pltpu.SMEM),
            pl.BlockSpec(memory_space=pltpu.HBM),
            pl.BlockSpec(memory_space=pltpu.HBM),
            pl.BlockSpec(memory_space=pltpu.HBM),
            pl.BlockSpec(memory_space=pltpu.HBM),
        ],
        out_specs=pl.BlockSpec(memory_space=vmem),
        scratch_shapes=[
            vmem((blocks, rb, columns), jnp.bfloat16),
            vmem((tok_rows, columns), jnp.bfloat16),
            vmem((tok_rows, columns), jnp.bfloat16),
            vmem(wo.shape, jnp.bfloat16),
            vmem((size * tok_rows, HEAD_DIM), jnp.bfloat16),
            vmem((size * tok_rows, HEAD_DIM), jnp.bfloat16),
            vmem((2, blocks, size * rb, HEAD_DIM), jnp.bfloat16),
            vmem((2, blocks, size * rb, HEAD_DIM), jnp.bfloat16),
            vmem((2, blocks, slabs, 2, HEAD_DIM), jnp.float32),
            vmem((2, blocks, rb, columns), jnp.bfloat16),
            vmem((2, blocks, head_count, 2, HEAD_DIM), jnp.float32),
            vmem((2, 2, stat_pad, HEAD_DIM), jnp.float32),
            vmem((blocks, rb, columns), jnp.bfloat16),
            vmem((sent, chunks, rb, chunk), jnp.float32),
            vmem((sent, chunks, rb, chunk), jnp.bfloat16),
            vmem((sent, chunks, rb, chunk), jnp.bfloat16),
            dma((2 + blocks,)),
            dma,
            dma((head_count,)),
            dma((head_count,)),
            dma((head_count,)),
            dma((blocks, head_count)),
            dma((size,)),
            dma((size,)),
            dma((size,)),
            dma((blocks, size)),
            dma((2, blocks, size)),
            dma((2, blocks, head_count)),
            dma((2, blocks, size)),
            dma((2, blocks, head_count)),
            dma((sent, chunks)),
            dma((sent, chunks)),
        ],
        compiler_params=pltpu.CompilerParams(
            collective_id=0, has_side_effects=True, vmem_limit_bytes=52 << 20
        ),
    )(*[pltpu.with_memory_space_constraint(x, pltpu.HBM) for x in (frame_tokens, queries, keys, values, wo)])


def solution(mesh):
    in_specs = (P("ctx", "tp"), P("ctx", "tp"), P("ctx", "tp"), P("tp", None), P())
    out_specs = P(("ctx", "tp"), None)
    return jax.shard_map(
        on_device, mesh=mesh, in_specs=in_specs, out_specs=out_specs, check_vma=False
    )
```

time: 28.6 us -> 27.5 us (0.962)
  the two profiles are of different devices: /device:TPU:16 before, /device:TPU:0 now
where the time goes in v1:
time: 27.5 us; the launch traced here: 27.3 us
  Pallas kernels  26.6 us (97%)
  local copies, waits for them, and re-layouts  0.68 us (2%)
    pallas_call x1, Pallas kernels, on_device(): pl.pallas_call(functools.partial(kernel, n, chunk), out_shape=jax.ShapeDt...  26.6 us
    unnamed x1, local copies, waits for them, and re-layouts  0.68 us

profile of v1, /device:TPU:0, one launch (start us, length us, event | category | flops | bytes accessed | tf_op | source)
XLA Modules:
  0.0 27.3 jit_solution(5223755717010745169)
XLA Ops:
  0.0 26.6 %shard_map.55 = bf16[32,3072]{1,0:T(8,128)(2,1)S(1)} custom-call(s32[16]{0:T(128)} %counts_ref.1, bf16[64,768]{1,0:T(8,128)(2,1)} %q_hbm.1, bf16[64,768]{1,0:T(8,128)(2,1)} %k_hbm.1, bf16[64,768]{1,0:T(8,128)(2,1)} %v_hbm.1, bf16[768,3072]{1,0:T(8,128)(2,1)} %wo_hbm.1), custom_call_target="tpu_custom_call" | custom-call | tf_op jit(solution)/shard_map/pallas_call | solution.py:547
  26.6 0.7 %copy.7 = bf16[32,3072]{1,0:T(8,128)(2,1)} copy(bf16[32,3072]{1,0:T(8,128)(2,1)S(1)} %shard_map.55) | data formatting | bytes 393216

commit v2 on v1

--- a/solution.py
+++ b/solution.py
@@ -108,7 +108,7 @@
         pltpu.make_async_copy(k_hbm, k_ref, in_sem.at[0]),
         pltpu.make_async_copy(v_hbm, v_ref, in_sem.at[1]),
     ] + [
-        pltpu.make_async_copy(q_hbm.at[pl.ds(start_of(b), rb), :], q_ref.at[b], in_sem.at[2 + b])
+        pltpu.make_async_copy(q_hbm.at[pl.ds(start_of(b), rb), :], q_ref.at[b], in_sem.at[2])
         for b in range(blocks)
     ]
     for load in loads:
@@ -136,25 +136,15 @@
                 greet(base + j, tp)
 
         each(size, other)
-
-    @pl.when(jnp.logical_not(is_host))
-    def _():
-        for place in places:
-            greet(base + place, tp)
-
-    expected = 1 + jnp.where(is_host, size - 1, head_count)
+        if split:
+
+            @pl.when(jnp.logical_not(is_upper))
+            def _():
+                each(size, lambda j: greet(size + j, tp))
+
+    expected = 1 + head_count - is_host.astype(jnp.int32)
     if split:
-
-        @pl.when(is_upper)
-        def _():
-            for place in places:
-                greet(place, tp)
-
-        @pl.when(jnp.logical_and(is_host, jnp.logical_not(is_upper)))
-        def _():
-            each(size, lambda j: greet(size + j, tp))
-
-        expected = expected + jnp.where(is_upper, head_count, jnp.where(is_host, size, 0))
+        expected = expected + jnp.where(is_upper, head_count, 0)
     with jax.named_scope("bar"):
         pl.semaphore_wait(barrier, expected)
 
@@ -172,40 +162,40 @@
 
     def give_k(h, frame, dev):
         return remote(
-            k_ref.at[:, head_cols[h]], k_in.at[rows_of(frame, tok_rows)], k_send.at[h], k_recv.at[frame], dev
+            k_ref.at[:, head_cols[h]], k_in.at[rows_of(frame, tok_rows)], k_send, k_recv, dev
         )
 
     def give_v(h, frame, dev):
         return remote(
-            v_ref.at[:, head_cols[h]], v_in.at[rows_of(frame, tok_rows)], v_send.at[h], v_recv.at[frame], dev
+            v_ref.at[:, head_cols[h]], v_in.at[rows_of(frame, tok_rows)], v_send, v_recv, dev
         )
 
     def give_q(h, frame, dev):
         return remote(
-            q_ref.at[:, :, head_cols[h]], q_in.at[NEAR, :, rows_of(frame, rb)], q_send.at[h], q_recv.at[frame], dev
+            q_ref.at[:, :, head_cols[h]], q_in.at[NEAR, :, rows_of(frame, rb)], q_send, q_recv, dev
         )
 
     def give_far(h, b, frame):
         return remote(
             q_ref.at[b, :, head_cols[h]],
             q_in.at[FAR, b, rows_of(frame, rb)],
-            far_send.at[b, h],
-            far_recv.at[b, frame],
+            far_send,
+            far_recv.at[b],
             places[h],
         )
 
     def own_copies():
         return (
-            pltpu.make_async_copy(k_ref.at[:, my_cols], k_in.at[rows_of(local, tok_rows)], k_recv.at[local]),
-            pltpu.make_async_copy(v_ref.at[:, my_cols], v_in.at[rows_of(local, tok_rows)], v_recv.at[local]),
+            pltpu.make_async_copy(k_ref.at[:, my_cols], k_in.at[rows_of(local, tok_rows)], k_recv),
+            pltpu.make_async_copy(v_ref.at[:, my_cols], v_in.at[rows_of(local, tok_rows)], v_recv),
             pltpu.make_async_copy(
-                q_ref.at[:, :, my_cols], q_in.at[NEAR, :, rows_of(local, rb)], q_recv.at[local]
+                q_ref.at[:, :, my_cols], q_in.at[NEAR, :, rows_of(local, rb)], q_recv
             ),
         )
 
     with jax.named_scope("own"):
-        for load in loads:
-            load.wait()
+        for ref, i in ((k_ref, 0), (v_ref, 1), (q_ref, 2)):
+            pltpu.make_async_copy(ref, ref, in_sem.at[i]).wait()
 
     def to_hosts(give):
         for h, place in enumerate(places):
@@ -214,31 +204,25 @@
             def _():
                 give(h, local, base + place).start()
 
-    if split:
-
-        @pl.when(is_upper)
-        def _():
-            for b in range(sent_blocks):
-                for h in range(head_count):
-                    give_far(h, b, local).start()
-
-    to_hosts(give_k)
-    to_hosts(give_v)
-    to_hosts(give_q)
+    def to_far(first, last):
+        if split:
+
+            @pl.when(is_upper)
+            def _():
+                for b in range(first, last):
+                    for h in range(head_count):
+                        give_far(h, b, local).start()
 
     @pl.when(is_host)
     def _():
         for copy in own_copies():
             copy.start()
 
-    if split:
-
-        @pl.when(is_upper)
-        def _():
-            for b in range(sent_blocks, blocks):
-                for h in range(head_count):
-                    give_far(h, b, local).start()
-
+    to_far(0, sent_blocks)
+    to_hosts(give_k)
+    to_hosts(give_q)
+    to_far(sent_blocks, blocks)
+    to_hosts(give_v)
     wo_copy.start()
 
     tile_frames = min(size, 256 // rb)
@@ -261,54 +245,53 @@
             limit = jnp.where(slot == f, counts_ref[base + kt * span_frames + f], limit)
         return place_in < limit
 
-    def attend(query, kind, first_frame):
-        def part(kt, old_max):
-            keys_at = rows_of(kt, span) if key_tiles > 1 else slice(0, span)
-            scores = lax.dot_general(
-                query, k_in[keys_at, :], (((1,), (1,)), ((), ())), preferred_element_type=jnp.float32
-            )
-            allowed = live_keys(kt)
-            if kind == NEAR:
-                allowed = jnp.logical_and(
-                    allowed, slot + kt * span_frames <= first_frame + tile_row // rb
-                )
-            scores = jnp.where(allowed, scores, NEG)
-            top = jnp.max(scores, axis=-1, keepdims=True)
-            if old_max is not None:
-                top = jnp.maximum(top, old_max)
-            weights = jnp.exp2((scores - top) * scale).astype(jnp.bfloat16)
-            added = jnp.dot(
-                weights,
-                jnp.concatenate([v_in[keys_at, :], ones], axis=1),
-                preferred_element_type=jnp.float32,
-            )
-            return top, added
-
-        top, acc = part(0, None)
-        if key_tiles > 1:
-
-            def more(kt, carry):
-                old_max, acc = carry
-                top, added = part(kt, old_max)
-                return top, jnp.exp2((old_max - top) * scale) * acc + added
-
-            top, acc = lax.fori_loop(1, key_tiles, more, (top, acc))
-        return top, acc
+    def weigh(query, kind, first_frame, kt, old_max):
+        keys_at = rows_of(kt, span) if key_tiles > 1 else slice(0, span)
+        scores = lax.dot_general(
+            query, k_in[keys_at, :], (((1,), (1,)), ((), ())), preferred_element_type=jnp.float32
+        )
+        allowed = live_keys(kt)
+        if kind == NEAR:
+            allowed = jnp.logical_and(allowed, slot + kt * span_frames <= first_frame + tile_row // rb)
+        scores = jnp.where(allowed, scores, NEG)
+        top = jnp.max(scores, axis=-1, keepdims=True)
+        if old_max is not None:
+            top = jnp.maximum(top, old_max)
+        return top, jnp.exp2((scores - top) * scale).astype(jnp.bfloat16)
+
+    def gather(weights, kt):
+        keys_at = rows_of(kt, span) if key_tiles > 1 else slice(0, span)
+        return jnp.dot(
+            weights,
+            jnp.concatenate([v_in[keys_at, :], ones], axis=1),
+            preferred_element_type=jnp.float32,
+        )
+
+    def more_keys(query, kind, first_frame, top, acc):
+        if key_tiles == 1:
+            return top, acc
+
+        def more(kt, carry):
+            old_max, acc = carry
+            top, weights = weigh(query, kind, first_frame, kt, old_max)
+            return top, jnp.exp2((old_max - top) * scale) * acc + gather(weights, kt)
+
+        return lax.fori_loop(1, key_tiles, more, (top, acc))
 
     def answer(kind, b, j, dev):
         return (
             remote(
                 acc_out.at[kind, b, rows_of(j, rb)],
                 acc_in.at[kind, b, :, my_cols],
-                acc_send.at[kind, b, j],
-                acc_recv.at[kind, b, my_head],
+                acc_send.at[kind],
+                acc_recv.at[kind, b],
                 dev,
             ),
             remote(
                 stat_out.at[kind, b, j // slab_frames],
                 stat_in.at[kind, b, my_head],
-                stat_send.at[kind, b, j],
-                stat_recv.at[kind, b, my_head],
+                stat_send.at[kind],
+                stat_recv.at[kind, b],
                 dev,
             ),
         )
@@ -318,86 +301,87 @@
             pltpu.make_async_copy(
                 acc_out.at[kind, b, rows_of(local, rb)],
                 acc_in.at[kind, b, :, my_cols],
-                acc_recv.at[kind, b, my_head],
+                acc_recv.at[kind, b],
             ),
             pltpu.make_async_copy(
                 stat_out.at[kind, b, local // slab_frames],
                 stat_in.at[kind, b, my_head],
-                stat_recv.at[kind, b, my_head],
+                stat_recv.at[kind, b],
             ),
         )
 
-    def serve(kind, b):
-        for t in range(size // tile_frames):
-            at = slice(t * tile_rows, (t + 1) * tile_rows)
-            top, acc = attend(q_in[kind, b, at, :], kind, t * tile_frames)
-            acc_out[kind, b, at, :] = acc[:, :HEAD_DIM].astype(jnp.bfloat16)
-            stats = jnp.where(lane == 0, top, acc[:, HEAD_DIM:])
-            for s in range(slabs):
-                turned = jnp.transpose(stats[s * HEAD_DIM : (s + 1) * HEAD_DIM])
-                stat_out[kind, b, t * slabs + s] = turned[:2]
-
-            def send(i):
-                j = t * tile_frames + i
-                if kind == NEAR:
-
-                    @pl.when(local != j)
-                    def _():
-                        for copy in answer(kind, b, j, base + j):
-                            copy.start()
-
-                    @pl.when(local == j)
-                    def _():
-                        for copy in keep_answer(kind, b):
-                            copy.start()
-
-                else:
-                    for copy in answer(kind, b, j, size + j):
+    tiles = size // tile_frames
+
+    def query_at(kind, b, t):
+        return q_in[kind, b, t * tile_rows : (t + 1) * tile_rows, :]
+
+    def begin(kind, b, t):
+        return weigh(query_at(kind, b, t), kind, t * tile_frames, 0, None)
+
+    def serve(kind, b, t, begun):
+        top, weights = begun
+        top, acc = more_keys(query_at(kind, b, t), kind, t * tile_frames, top, gather(weights, 0))
+        acc_out[kind, b, t * tile_rows : (t + 1) * tile_rows, :] = acc[:, :HEAD_DIM].astype(jnp.bfloat16)
+        stats = jnp.where(lane == 0, top, acc[:, HEAD_DIM:])
+        for s in range(slabs):
+            turned = jnp.transpose(stats[s * HEAD_DIM : (s + 1) * HEAD_DIM])
+            stat_out[kind, b, t * slabs + s] = turned[:2]
+
+        def send(i):
+            j = (t + 1) * tile_frames - 1 - i
+            if kind == NEAR:
+
+                @pl.when(local != j)
+                def _():
+                    for copy in answer(kind, b, j, base + j):
                         copy.start()
 
-            each(tile_frames, send)
+                @pl.when(local == j)
+                def _():
+                    for copy in keep_answer(kind, b):
+                        copy.start()
+
+            else:
+                for copy in answer(kind, b, j, size + j):
+                    copy.start()
+
+        each(tile_frames, send)
+
+    def arrived(ref, sem):
+        pltpu.make_async_copy(ref, ref, sem).wait()
 
     @pl.when(is_host)
     def _():
         with jax.named_scope("wk"):
-            each(size, lambda j: give_k(0, j, me).wait_recv())
+            arrived(k_in, k_recv)
+        with jax.named_scope("wq"):
+            arrived(q_in.at[NEAR], q_recv)
+        first = tiles == 1 and key_tiles == 1
+        with jax.named_scope("beg"):
+            begun = [begin(NEAR, b, 0) for b in range(blocks)] if first else None
         with jax.named_scope("wv"):
-            each(size, lambda j: give_v(0, j, me).wait_recv())
+            arrived(v_in, v_recv)
+        with jax.named_scope("sn"):
+            for b in range(blocks):
+                for t in range(tiles):
+                    serve(NEAR, b, t, begun[b] if first else begin(NEAR, b, t))
         if split:
 
             @pl.when(jnp.logical_not(is_upper))
             def _():
                 for b in range(blocks):
                     with jax.named_scope("wf"):
-                        each(size, lambda j: give_far(0, b, j).wait_recv())
+                        arrived(q_in.at[FAR, b], far_recv.at[b])
                     with jax.named_scope("sf"):
-                        serve(FAR, b)
-
-        with jax.named_scope("wq"):
-            each(size, lambda j: give_q(0, j, me).wait_recv())
-        for b in range(blocks):
-            with jax.named_scope("sn"):
-                serve(NEAR, b)
+                        for t in range(tiles):
+                            serve(FAR, b, t, begin(FAR, b, t))
 
     row = lax.broadcasted_iota(jnp.int32, (rb, HEAD_DIM), 0)
     padding = jnp.zeros((HEAD_DIM - 2 * stat_rows.shape[2], HEAD_DIM), jnp.float32)
 
     def wait_answers(kind, b):
-        for h in range(head_count):
-            remote(
-                acc_out.at[kind, b, rows_of(0, rb)],
-                acc_in.at[kind, b, :, head_cols[h]],
-                acc_send.at[kind, b, 0],
-                acc_recv.at[kind, b, h],
-                me,
-            ).wait_recv()
-            remote(
-                stat_out.at[kind, b, 0],
-                stat_in.at[kind, b, h],
-                stat_send.at[kind, b, 0],
-                stat_recv.at[kind, b, h],
-                me,
-            ).wait_recv()
+        arrived(acc_in.at[kind, b], acc_recv.at[kind, b])
+        arrived(stat_in.at[kind, b], stat_recv.at[kind, b])
 
     def stats_of(kind, b):
         for h in range(head_count):
@@ -427,7 +411,7 @@
         return pltpu.make_async_remote_copy(
             src_ref=outgoing.at[b, c],
             dst_ref=incoming.at[b, c],
-            send_sem=x_send_sem.at[b, c],
+            send_sem=x_send_sem,
             recv_sem=x_recv_sem.at[b, c],
             device_id=(me, 1 - tp),
             device_id_type=MESH,
@@ -476,44 +460,39 @@
                 else:
                     kept[b - sent_blocks, c] = part
 
+    def left(ref, sem):
+        pltpu.make_async_copy(ref, ref, sem).wait()
+
+    def answers_left(kind, count):
+        left(acc_out.at[kind, :, : count * rb], acc_send.at[kind])
+        bits = stat_out.shape[3] * 2
+        left(acc_out.at[kind, :, : count * bits], stat_send.at[kind])
+
     with jax.named_scope("drain"):
-        for h, place in enumerate(places):
-
-            @pl.when(local != place)
-            def _():
-                give_k(h, local, base + place).wait_send()
-                give_v(h, local, base + place).wait_send()
-                give_q(h, local, base + place).wait_send()
-
-        if split:
-
-            @pl.when(is_upper)
-            def _():
-                for b in range(blocks):
-                    for h in range(head_count):
-                        give_far(h, b, local).wait_send()
-
-            @pl.when(jnp.logical_and(is_host, jnp.logical_not(is_upper)))
-            def _():
-                for b in range(blocks):
-
-                    def drain_far(j):
-                        for copy in answer(FAR, b, j, size + j):
-                            copy.wait_send()
-
-                    each(size, drain_far)
+
+        def gifts_left(count):
+            left(k_ref.at[:, : count * HEAD_DIM], k_send)
+            left(v_ref.at[:, : count * HEAD_DIM], v_send)
+            left(q_ref.at[:, :, : count * HEAD_DIM], q_send)
 
         @pl.when(is_host)
         def _():
-            for b in range(blocks):
-
-                def drain_near(j):
-                    @pl.when(local != j)
-                    def _():
-                        for copy in answer(NEAR, b, j, base + j):
-                            copy.wait_send()
-
-                each(size, drain_near)
+            gifts_left(head_count - 1)
+            answers_left(NEAR, size - 1)
+
+        @pl.when(jnp.logical_not(is_host))
+        def _():
+            gifts_left(head_count)
+
+        if split:
+
+            @pl.when(is_upper)
+            def _():
+                left(q_ref, far_send)
+
+            @pl.when(jnp.logical_and(is_host, jnp.logical_not(is_upper)))
+            def _():
+                answers_left(FAR, size)
 
     for b in range(sent_blocks):
         for c in range(width // chunk):
@@ -523,9 +502,7 @@
                 kept[b, c] + incoming[b, c].astype(jnp.float32)
             ).astype(out_ref.dtype)
     with jax.named_scope("fin"):
-        for b in range(sent_blocks):
-            for c in range(width // chunk):
-                swap(b, c).wait_send()
+        left(outgoing, x_send_sem)
 
 
 def on_device(queries, keys, values, wo, frame_tokens):
@@ -572,21 +549,21 @@
             vmem((sent, chunks, rb, chunk), jnp.float32),
             vmem((sent, chunks, rb, chunk), jnp.bfloat16),
             vmem((sent, chunks, rb, chunk), jnp.bfloat16),
-            dma((2 + blocks,)),
-            dma,
-            dma((head_count,)),
-            dma((head_count,)),
-            dma((head_count,)),
-            dma((blocks, head_count)),
-            dma((size,)),
-            dma((size,)),
-            dma((size,)),
-            dma((blocks, size)),
-            dma((2, blocks, size)),
-            dma((2, blocks, head_count)),
-            dma((2, blocks, size)),
-            dma((2, blocks, head_count)),
-            dma((sent, chunks)),
+            dma((3,)),
+            dma,
+            dma,
+            dma,
+            dma,
+            dma,
+            dma,
+            dma,
+            dma,
+            dma((blocks,)),
+            dma((2,)),
+            dma((2, blocks)),
+            dma((2,)),
+            dma((2, blocks)),
+            dma,
             dma((sent, chunks)),
         ],
         compiler_params=pltpu.CompilerParams(

time: 27.5 us -> 24.1 us (0.88)
  the two profiles are of different devices: /device:TPU:0 before, /device:TPU:16 now
where the time goes in v2:
time: 24.1 us; the launch traced here: 23.9 us
  Pallas kernels  23.2 us (96%)
  local copies, waits for them, and re-layouts  0.68 us (3%)
    pallas_call x1, Pallas kernels, on_device(): pl.pallas_call(functools.partial(kernel, n, chunk), out_shape=jax.ShapeDt...  23.2 us
    unnamed x1, local copies, waits for them, and re-layouts  0.68 us

profile of v2, /device:TPU:16, one launch (start us, length us, event | category | flops | bytes accessed | tf_op | source)
XLA Modules:
  0.0 23.9 jit_solution(5813758737284267983)
XLA Ops:
  0.0 23.2 %shard_map.55 = bf16[32,3072]{1,0:T(8,128)(2,1)S(1)} custom-call(s32[16]{0:T(128)} %counts_ref.1, bf16[64,768]{1,0:T(8,128)(2,1)} %q_hbm.1, bf16[64,768]{1,0:T(8,128)(2,1)} %k_hbm.1, bf16[64,768]{1,0:T(8,128)(2,1)} %v_hbm.1, bf16[768,3072]{1,0:T(8,128)(2,1)} %wo_hbm.1), custom_call_target="tpu_custom_call" | custom-call | tf_op jit(solution)/shard_map/pallas_call | solution.py:524
  23.2 0.7 %copy.7 = bf16[32,3072]{1,0:T(8,128)(2,1)} copy(bf16[32,3072]{1,0:T(8,128)(2,1)S(1)} %shard_map.55) | data formatting | bytes 393216

commit v3 on v2

v3 whole, which is shorter than its diff:
```python
import functools
import math

import jax
import jax.numpy as jnp
from jax import lax
from jax.experimental import pallas as pl
from jax.experimental.pallas import tpu as pltpu
from jax.sharding import PartitionSpec as P

HEAD_DIM = 128
LAYER = 4
NEG = -1e30
MESH = pl.DeviceIdType.MESH
FAR, NEAR = 0, 1
STAT_ROWS = 8


def group_size(n):
    levels = n // LAYER
    return n // 2 if levels % 2 == 0 else n


def host_places(size, head_count):
    top = size - LAYER
    order = [top + i for i in (0, 2, 1, 3)] + list(range(top))
    return order[:head_count]


def kernel(
    n,
    chunk,
    counts_ref,
    q_hbm,
    k_hbm,
    v_hbm,
    wo_hbm,
    out_ref,
    q_ref,
    k_pal,
    v_pal,
    wo_all,
    k_in,
    v_in,
    q_in,
    acc_out,
    stat_out,
    acc_in,
    stat_in,
    stat_rows,
    near_stat,
    attended,
    kept,
    outgoing,
    incoming,
    in_sem,
    wo_sem,
    k_send,
    v_send,
    q_send,
    far_send,
    k_recv,
    v_recv,
    q_recv,
    far_recv,
    pal_send,
    pal_recv,
    acc_send,
    acc_recv,
    stat_send,
    stat_recv,
    x_send_sem,
    x_recv_sem,
):
    tok_rows, columns = k_hbm.shape
    head_count = columns // HEAD_DIM
    width = wo_hbm.shape[1]
    half = tok_rows // 2
    quarter = half // 2
    chunks = width // chunk
    parts = [(0, quarter), (quarter, quarter), (half, half)]
    me = lax.axis_index("ctx")
    tp = lax.axis_index("tp")
    size = group_size(n)
    split = size < n
    upper = me // size
    base = upper * size
    local = me - base
    is_upper = upper > 0
    is_lower = jnp.logical_not(is_upper)
    is_base = local < LAYER
    is_top = jnp.logical_not(is_base)
    lane = lax.rem(me, LAYER)
    places = host_places(size, head_count)
    my_head = jnp.int32(0)
    is_host = local < 0
    for h, place in enumerate(places):
        my_head = jnp.where(local == place, h, my_head)
        is_host = jnp.logical_or(is_host, local == place)
    my_cols = pl.ds(pl.multiple_of(my_head * HEAD_DIM, HEAD_DIM), HEAD_DIM)
    head_cols = [slice(h * HEAD_DIM, (h + 1) * HEAD_DIM) for h in range(head_count)]
    scale = math.log2(math.e) / math.sqrt(HEAD_DIM)

    def both(a, b):
        return jnp.logical_and(a, b)

    def start_of(b):
        return pl.multiple_of((1 - tp if b == 0 else tp) * half, half)

    def rows_of(src, rows):
        return pl.ds(pl.multiple_of(src * rows, rows), rows)

    pltpu.make_async_copy(k_hbm, k_pal.at[lane], in_sem.at[0]).start()
    pltpu.make_async_copy(v_hbm, v_pal.at[lane], in_sem.at[1]).start()
    for b in range(2):
        pltpu.make_async_copy(q_hbm.at[pl.ds(start_of(b), half), :], q_ref.at[b], in_sem.at[2]).start()

    wo_copy = pltpu.make_async_copy(wo_hbm, wo_all, wo_sem)
    first_pair = both(both(is_base, is_lower), lane < 2)
    pl.when(first_pair)(wo_copy.start)
    barrier = pltpu.get_barrier_semaphore()

    def greet(dev, other_tp):
        pl.semaphore_signal(barrier, inc=1, device_id=(dev, other_tp), device_id_type=MESH)

    def each(count, body):
        if count <= 16:
            for j in range(count):
                body(j)
        else:
            lax.fori_loop(0, count, lambda j, carry: (body(j), carry)[1], 0)

    greet(me, 1 - tp)
    takes = {1: (0,), 2: (0, 3), 3: (1, 2)}
    for to, sources in takes.items():

        @pl.when(both(is_base, lane == to))
        def _():
            for source in sources:
                greet(base + source, tp)

    @pl.when(is_host)
    def _():
        def other(j):
            @pl.when(local != j)
            def _():
                greet(base + j, tp)

        each(size, other)
        if split:

            @pl.when(is_lower)
            def _():
                each(size, lambda j: greet(size + j, tp))

    gifts = jnp.where(lane == 0, 2, 1)
    expected = 1 + head_count - is_host.astype(jnp.int32) + jnp.where(is_base, gifts, 0)
    if split:
        expected = expected + jnp.where(is_upper, head_count, 0)
    with jax.named_scope("bar"):
        pl.semaphore_wait(barrier, expected)

    def remote(src, dst, send, recv, dev):
        return pltpu.make_async_remote_copy(
            src_ref=src,
            dst_ref=dst,
            send_sem=send,
            recv_sem=recv,
            device_id=(dev, tp),
            device_id_type=MESH,
        )

    def arrived(ref, sem):
        pltpu.make_async_copy(ref, ref, sem).wait()

    def give_k(h, dev):
        return remote(k_pal.at[lane, :, head_cols[h]], k_in.at[rows_of(local, tok_rows)], k_send, k_recv, dev)

    def give_v(h, dev):
        return remote(v_pal.at[lane, :, head_cols[h]], v_in.at[rows_of(local, tok_rows)], v_send, v_recv, dev)

    def give_q(h, dev):
        return remote(q_ref.at[:, :, head_cols[h]], q_in.at[NEAR, :, rows_of(local, half)], q_send, q_recv, dev)

    def give_far(h, b):
        return remote(
            q_ref.at[b, :, head_cols[h]],
            q_in.at[FAR, b, rows_of(local, half)],
            far_send,
            far_recv.at[b],
            places[h],
        )

    def pal(kind, frame, to):
        ref = (k_pal, v_pal)[kind].at[frame]
        return remote(ref, ref, pal_send, pal_recv.at[kind, frame], base + to)

    with jax.named_scope("own"):
        arrived(k_pal.at[lane], in_sem.at[0])
        arrived(v_pal.at[lane], in_sem.at[1])
        arrived(q_ref, in_sem.at[2])

    def to_hosts(give):
        for h in nearest_last:
            place = places[h]

            @pl.when(local != place)
            def _():
                give(h, base + place).start()

    nearest_last = sorted(range(head_count), key=lambda h: places[h])

    def to_far(b, who):
        if split:

            @pl.when(both(is_upper, who))
            def _():
                for h in nearest_last:
                    give_far(h, b).start()

    @pl.when(both(is_base, lane == 0))
    def _():
        for kind in range(2):
            pal(kind, 0, 1).start()

    @pl.when(both(is_base, lane == 2))
    def _():
        for kind in range(2):
            pal(kind, 2, 3).start()

    to_far(0, is_upper)
    to_far(1, is_base)
    to_hosts(give_k)

    @pl.when(both(is_upper, is_top))
    def _():
        to_hosts(give_q)

    to_hosts(give_v)
    to_far(1, is_top)

    @pl.when(is_host)
    def _():
        pltpu.make_async_copy(k_pal.at[lane, :, my_cols], k_in.at[rows_of(local, tok_rows)], k_recv).start()
        pltpu.make_async_copy(v_pal.at[lane, :, my_cols], v_in.at[rows_of(local, tok_rows)], v_recv).start()

        @pl.when(is_top)
        def _():
            pltpu.make_async_copy(
                q_ref.at[:, :, my_cols], q_in.at[NEAR, :, rows_of(local, half)], q_recv
            ).start()

    @pl.when(both(is_lower, is_top))
    def _():
        to_hosts(give_q)

    for kind in range(2):
        for source in range(2):

            @pl.when(both(is_base, lane == source))
            def _():
                pal(kind, source, source + 2).start()

    pl.when(jnp.logical_not(first_pair))(wo_copy.start)

    def masked_weights(scores, allowed):
        scores = jnp.where(allowed, scores, NEG)
        top = jnp.max(scores, axis=-1, keepdims=True)
        return top, jnp.exp2((scores - top) * scale).astype(jnp.bfloat16)

    def attend_level():
        col = lax.broadcasted_iota(jnp.int32, (1, LAYER * tok_rows), 1)
        slot = col // tok_rows
        limit = jnp.zeros(col.shape, jnp.int32)
        for f in range(LAYER):
            limit = jnp.where(slot == f, jnp.where(f <= lane, counts_ref[base + f], 0), limit)
        allowed = lax.rem(col, tok_rows) < limit
        ones = jnp.ones((LAYER * tok_rows, HEAD_DIM), jnp.bfloat16)
        frames = [jnp.minimum(f, lane) for f in range(LAYER)]
        at = lax.broadcasted_iota(jnp.int32, (tok_rows, HEAD_DIM), 1)
        begun = []
        for cols in head_cols:
            query = jnp.concatenate([q_ref[0, :, cols], q_ref[1, :, cols]], axis=0)
            keys = jnp.concatenate([k_pal[f, :, cols] for f in frames], axis=0)
            scores = lax.dot_general(
                query, keys, (((1,), (1,)), ((), ())), preferred_element_type=jnp.float32
            )
            begun.append(masked_weights(scores, allowed))
        stats = jnp.zeros((tok_rows, HEAD_DIM), jnp.float32)
        for h, cols in enumerate(head_cols):
            top, weights = begun[h]
            vals = jnp.concatenate([v_pal[f, :, cols] for f in frames], axis=0)
            acc = jnp.dot(weights, jnp.concatenate([vals, ones], axis=1), preferred_element_type=jnp.float32)
            acc_in[NEAR, :, cols] = acc[:, :HEAD_DIM].astype(jnp.bfloat16)
            stats = jnp.where(at == h, top, stats)
            stats = jnp.where(at == STAT_ROWS + h, acc[:, HEAD_DIM:], stats)
        near_stat[:tok_rows, :] = stats

    far_frames = min(size, 256 // half)
    near_frames = min(size - LAYER, HEAD_DIM // half)
    slab_frames = HEAD_DIM // half
    span_frames = min(size, 8)
    span = span_frames * tok_rows
    key_tiles = size // span_frames
    col = lax.broadcasted_iota(jnp.int32, (1, span), 1)
    slot = col // tok_rows
    place_in = lax.rem(col, tok_rows)
    ones = jnp.ones((span, HEAD_DIM), jnp.bfloat16)

    def keys_at(kt):
        return rows_of(kt, span) if key_tiles > 1 else slice(0, span)

    def weigh(query, row_frame, kt, old_max):
        scores = lax.dot_general(
            query, k_in[keys_at(kt), :], (((1,), (1,)), ((), ())), preferred_element_type=jnp.float32
        )
        limit = jnp.zeros((1, span), jnp.int32)
        for f in range(span_frames):
            limit = jnp.where(slot == f, counts_ref[base + kt * span_frames + f], limit)
        allowed = place_in < limit
        if row_frame is not None:
            allowed = jnp.logical_and(allowed, slot + kt * span_frames <= row_frame)
        scores = jnp.where(allowed, scores, NEG)
        top = jnp.max(scores, axis=-1, keepdims=True)
        if old_max is not None:
            top = jnp.maximum(top, old_max)
        return top, jnp.exp2((scores - top) * scale).astype(jnp.bfloat16)

    def gather(weights, kt):
        return jnp.dot(
            weights,
            jnp.concatenate([v_in[keys_at(kt), :], ones], axis=1),
            preferred_element_type=jnp.float32,
        )

    def more_keys(query, row_frame, top, acc):
        if key_tiles == 1:
            return top, acc

        def more(kt, carry):
            old_max, acc = carry
            top, weights = weigh(query, row_frame, kt, old_max)
            return top, jnp.exp2((old_max - top) * scale) * acc + gather(weights, kt)

        return lax.fori_loop(1, key_tiles, more, (top, acc))

    def begin(query, row_frame):
        return query, row_frame, weigh(query, row_frame, 0, None)

    def end(begun):
        query, row_frame, (top, weights) = begun
        return more_keys(query, row_frame, top, gather(weights, 0))

    def acc_copies(kind, p, j, dev):
        first, rows = parts[p]
        b = first // half
        src = acc_out.at[kind, b, pl.ds(j * half + first - b * half, rows)]
        dst = acc_in.at[kind, pl.ds(first, rows), my_cols]
        return src, dst, acc_send.at[kind], acc_recv.at[kind, p], dev

    def stat_copies(kind, b, j, dev):
        return (
            stat_out.at[kind, b, j // slab_frames],
            stat_in.at[kind, b, my_head],
            stat_send.at[kind],
            stat_recv.at[kind, b],
            dev,
        )

    def post(kind, copy, frames):
        for j in frames:
            if kind == FAR:
                remote(*copy(j, size + j)).start()
            else:
                src, dst, send, recv, dev = copy(j, base + j)

                @pl.when(local != j)
                def _():
                    remote(src, dst, send, recv, dev).start()

                @pl.when(local == j)
                def _():
                    pltpu.make_async_copy(src, dst, recv).start()

    def stats_from(kind, b, first, top, acc):
        at = lax.broadcasted_iota(jnp.int32, acc[:, HEAD_DIM:].shape, 1)
        stats = jnp.where(at == 0, top, acc[:, HEAD_DIM:])
        for s in range(stats.shape[0] // HEAD_DIM):
            turned = jnp.transpose(stats[s * HEAD_DIM : (s + 1) * HEAD_DIM])
            stat_out[kind, b, first // slab_frames + s] = turned[:2]

    def begin_far(b, t):
        return begin(q_in[FAR, b, t * far_frames * half : (t + 1) * far_frames * half, :], None)

    def serve_far(b, t, begun):
        top, acc = end(begun)
        first = t * far_frames
        acc_out[FAR, b, first * half : (first + far_frames) * half, :] = acc[:, :HEAD_DIM].astype(jnp.bfloat16)
        frames = range(first + far_frames - 1, first - 1, -1)
        mine = [p for p, (at, rows) in enumerate(parts) if at // half == b]
        post(FAR, lambda j, dev: acc_copies(FAR, mine[0], j, dev), frames)
        stats_from(FAR, b, first, top, acc)
        post(FAR, lambda j, dev: stat_copies(FAR, b, j, dev), frames)
        for p in mine[1:]:
            post(FAR, lambda j, dev: acc_copies(FAR, p, j, dev), frames)

    near_rows = near_frames * half
    near_tiles = (size - LAYER) // near_frames

    def near_at(t):
        first = LAYER + t * near_frames
        return first, slice(first * half, (first + near_frames) * half)

    def begin_near(t):
        first, at = near_at(t)
        row = lax.broadcasted_iota(jnp.int32, (2 * near_rows, 1), 0)
        query = jnp.concatenate([q_in[NEAR, 0, at, :], q_in[NEAR, 1, at, :]], axis=0)
        return begin(query, first + lax.rem(row, near_rows) // half)

    def serve_near(t, begun):
        top, acc = end(begun)
        first, at = near_at(t)
        for b in range(2):
            rows = slice(b * near_rows, (b + 1) * near_rows)
            acc_out[NEAR, b, at, :] = acc[rows, :HEAD_DIM].astype(jnp.bfloat16)
        frames = range(first + near_frames - 1, first - 1, -1)
        post(NEAR, lambda j, dev: acc_copies(NEAR, 0, j, dev), frames)
        for b in range(2):
            rows = slice(b * near_rows, (b + 1) * near_rows)
            stats_from(NEAR, b, first, top[rows], acc[rows])
            post(NEAR, lambda j, dev: stat_copies(NEAR, b, j, dev), frames)
        for p in (1, 2):
            post(NEAR, lambda j, dev: acc_copies(NEAR, p, j, dev), frames)

    def serve_all_near(begun):
        with jax.named_scope("sn"):
            for t in range(near_tiles):
                serve_near(t, begun if begun is not None else begin_near(t))

    def serve_all_far(b, begun):
        with jax.named_scope("sf"):
            for t in range(size // far_frames):
                serve_far(b, t, begun if begun is not None else begin_far(b, t))

    def host():
        with jax.named_scope("wk"):
            arrived(k_in, k_recv)

        def wait_near():
            with jax.named_scope("wq"):
                arrived(q_in.at[NEAR, :, LAYER * half :], q_recv)

        def host_near():
            wait_near()
            with jax.named_scope("bn"):
                begun = begin_near(0) if near_tiles == 1 and key_tiles == 1 else None
            with jax.named_scope("wv"):
                arrived(v_in, v_recv)
            serve_all_near(begun)

        def host_both():
            with jax.named_scope("wf"):
                arrived(q_in.at[FAR, 0], far_recv.at[0])
            with jax.named_scope("bf"):
                begun = begin_far(0, 0) if size == far_frames and key_tiles == 1 else None
            with jax.named_scope("wv"):
                arrived(v_in, v_recv)
            serve_all_far(0, begun)
            wait_near()
            serve_all_near(None)
            with jax.named_scope("wf"):
                arrived(q_in.at[FAR, 1], far_recv.at[1])
            serve_all_far(1, None)

        if split:
            pl.when(is_lower)(host_both)
            pl.when(is_upper)(host_near)
        else:
            host_near()

    lead = lax.rem(local, slab_frames) * half
    row = lax.broadcasted_iota(jnp.int32, (half, HEAD_DIM), 0)
    padding = jnp.zeros((HEAD_DIM - 2 * STAT_ROWS, HEAD_DIM), jnp.float32)

    def stat_columns(kind, b):
        for h in range(head_count):
            stat_rows[kind, h : h + 1, :] = stat_in[kind, b, h, 0:1, :]
            stat_rows[kind, STAT_ROWS + h : STAT_ROWS + h + 1, :] = stat_in[kind, b, h, 1:2, :]
        turned = jnp.transpose(jnp.concatenate([stat_rows[kind], padding], axis=0))
        picked = turned[:half]
        for i in range(1, slab_frames):
            picked = jnp.where(lead == i * half, turned[i * half : (i + 1) * half], picked)
        return picked

    def sums(stats):
        return pltpu.roll(stats, HEAD_DIM - STAT_ROWS, 1)

    def swap(p, c):
        first, rows = parts[p]
        return pltpu.make_async_remote_copy(
            src_ref=outgoing.at[p, c],
            dst_ref=incoming.at[p, c],
            send_sem=x_send_sem,
            recv_sem=x_recv_sem.at[p, c],
            device_id=(me, 1 - tp),
            device_id_type=MESH,
        )

    def own_rows(which, from_hosts, from_far):
        for p in which:
            first, rows = parts[p]
            b = first // half
            if from_hosts:

                @pl.when(is_top)
                def _():
                    with jax.named_scope("wan"):
                        arrived(acc_in.at[NEAR, pl.ds(first, rows)], acc_recv.at[NEAR, p])
                        if first % half == 0:
                            arrived(stat_in.at[NEAR, b], stat_recv.at[NEAR, b])
                            near_stat[b * half : (b + 1) * half, :] = stat_columns(NEAR, b)

            live = row[:rows] + (start_of(b) + first - b * half) < counts_ref[me]

            def merge(far):
                near = near_stat[first : first + rows, :]
                if far:
                    other = near_stat[tok_rows + first : tok_rows + first + rows, :]
                    top = jnp.maximum(near, other)
                    near_part = jnp.exp2((near - top) * scale)
                    far_part = jnp.exp2((other - top) * scale)
                    total = near_part * sums(near) + far_part * sums(other)
                    factors = ((NEAR, near_part / total), (FAR, far_part / total))
                else:
                    factors = ((NEAR, 1.0 / sums(near)),)
                for h, cols in enumerate(head_cols):
                    out = 0.0
                    for kind, factor in factors:
                        out = out + factor[:, h : h + 1] * acc_in[kind, first : first + rows, cols].astype(
                            jnp.float32
                        )
                    attended[first : first + rows, cols] = jnp.where(live, out, 0.0).astype(jnp.bfloat16)

            if from_far:

                @pl.when(is_upper)
                def _():
                    with jax.named_scope("waf"):
                        arrived(acc_in.at[FAR, pl.ds(first, rows)], acc_recv.at[FAR, p])
                        if first % half == 0:
                            arrived(stat_in.at[FAR, b], stat_recv.at[FAR, b])
                            near_stat[tok_rows + b * half : tok_rows + (b + 1) * half, :] = stat_columns(FAR, b)
                    merge(True)

                @pl.when(is_lower)
                def _():
                    merge(False)

            else:
                merge(False)

            if p == 0:
                wo_copy.wait()
            with jax.named_scope("proj"):
                lhs = attended[first : first + rows, :]
                for c in range(chunks):
                    part = jnp.dot(
                        lhs, wo_all[:, c * chunk : (c + 1) * chunk], preferred_element_type=jnp.float32
                    )
                    if b == 0:
                        outgoing[p, c] = part.astype(jnp.bfloat16)
                        swap(p, c).start()
                    else:
                        kept[:, c * chunk : (c + 1) * chunk] = part

    @pl.when(is_base)
    def _():
        def pass_on(frame, to):
            for kind in range(2):
                arrived((k_pal, v_pal)[kind].at[frame], pal_recv.at[kind, frame])
                if to is not None:
                    pal(kind, frame, to).start()

        with jax.named_scope("pal"):

            @pl.when(lane == 1)
            def _():
                pass_on(0, None)

            @pl.when(lane == 2)
            def _():
                pass_on(0, 3)
                pass_on(1, None)

            @pl.when(lane == 3)
            def _():
                pass_on(1, 2)
                pass_on(2, None)
                pass_on(0, None)

        with jax.named_scope("lev"):
            attend_level()

        @pl.when(is_lower)
        def _():
            own_rows((0,), False, False)

    pl.when(is_host)(host)

    @pl.when(both(is_base, is_lower))
    def _():
        own_rows((1, 2), False, False)

    @pl.when(jnp.logical_not(both(is_base, is_lower)))
    def _():
        own_rows((0, 1, 2), True, split)

    with jax.named_scope("drain"):

        def given(count):
            arrived(k_pal.at[0, :, : count * HEAD_DIM], k_send)
            arrived(v_pal.at[0, :, : count * HEAD_DIM], v_send)

            @pl.when(is_top)
            def _():
                arrived(q_ref.at[:, :, : count * HEAD_DIM], q_send)

        def answered(kind, count):
            arrived(acc_out.at[kind, :, : count * half], acc_send.at[kind])
            arrived(acc_out.at[kind, :, : count * 4], stat_send.at[kind])

        @pl.when(is_host)
        def _():
            given(head_count - 1)

            @pl.when(is_top)
            def _():
                answered(NEAR, size - LAYER - 1)

            @pl.when(is_base)
            def _():
                answered(NEAR, size - LAYER)

            if split:

                @pl.when(is_lower)
                def _():
                    answered(FAR, size)

        @pl.when(jnp.logical_not(is_host))
        def _():
            given(head_count)

        if split:

            @pl.when(is_upper)
            def _():
                arrived(q_ref, far_send)

        for lanes, count in (((0, 2), 2), ((1, 3), 1)):

            @pl.when(both(is_base, jnp.logical_or(lane == lanes[0], lane == lanes[1])))
            def _():
                arrived(k_pal.at[: 2 * count], pal_send)

    for c in range(chunks):
        at = slice(c * chunk, (c + 1) * chunk)
        for p in range(2):
            first, rows = parts[p]
            with jax.named_scope("swapw"):
                arrived(incoming.at[p, c], x_recv_sem.at[p, c])
            out_ref[first : first + rows, at] = (
                kept[first : first + rows, at] + incoming[p, c].astype(jnp.float32)
            ).astype(out_ref.dtype)
    with jax.named_scope("fin"):
        arrived(outgoing, x_send_sem)


def on_device(queries, keys, values, wo, frame_tokens):
    tok_rows, columns = queries.shape
    width = wo.shape[1]
    n = lax.axis_size("ctx")
    half = tok_rows // 2
    chunk = 512 if width % 512 == 0 else width
    chunks = width // chunk
    head_count = columns // HEAD_DIM
    size = group_size(n)
    slabs = size * half // HEAD_DIM
    vmem = pltpu.VMEM
    dma = pltpu.SemaphoreType.DMA
    return pl.pallas_call(
        functools.partial(kernel, n, chunk),
        out_shape=jax.ShapeDtypeStruct((half, width), jnp.bfloat16),
        in_specs=[
            pl.BlockSpec(memory_space=pltpu.SMEM),
            pl.BlockSpec(memory_space=pltpu.HBM),
            pl.BlockSpec(memory_space=pltpu.HBM),
            pl.BlockSpec(memory_space=pltpu.HBM),
            pl.BlockSpec(memory_space=pltpu.HBM),
        ],
        out_specs=pl.BlockSpec(memory_space=vmem),
        scratch_shapes=[
            vmem((2, half, columns), jnp.bfloat16),
            vmem((LAYER, tok_rows, columns), jnp.bfloat16),
            vmem((LAYER, tok_rows, columns), jnp.bfloat16),
            vmem(wo.shape, jnp.bfloat16),
            vmem((size * tok_rows, HEAD_DIM), jnp.bfloat16),
            vmem((size * tok_rows, HEAD_DIM), jnp.bfloat16),
            vmem((2, 2, size * half, HEAD_DIM), jnp.bfloat16),
            vmem((2, 2, size * half, HEAD_DIM), jnp.bfloat16),
            vmem((2, 2, slabs, 2, HEAD_DIM), jnp.float32),
            vmem((2, tok_rows, columns), jnp.bfloat16),
            vmem((2, 2, head_count, 2, HEAD_DIM), jnp.float32),
            vmem((2, 2 * STAT_ROWS, HEAD_DIM), jnp.float32),
            vmem((2 * tok_rows, HEAD_DIM), jnp.float32),
            vmem((tok_rows, columns), jnp.bfloat16),
            vmem((half, width), jnp.float32),
            vmem((2, chunks, half // 2, chunk), jnp.bfloat16),
            vmem((2, chunks, half // 2, chunk), jnp.bfloat16),
            dma((3,)),
            dma,
            dma,
            dma,
            dma,
            dma,
            dma,
            dma,
            dma,
            dma((2,)),
            dma,
            dma((2, LAYER - 1)),
            dma((2,)),
            dma((2, 3)),
            dma((2,)),
            dma((2, 2)),
            dma,
            dma((2, chunks)),
        ],
        compiler_params=pltpu.CompilerParams(
            collective_id=0, has_side_effects=True, vmem_limit_bytes=52 << 20
        ),
    )(*[pltpu.with_memory_space_constraint(x, pltpu.HBM) for x in (frame_tokens, queries, keys, values, wo)])


def solution(mesh):
    in_specs = (P("ctx", "tp"), P("ctx", "tp"), P("ctx", "tp"), P("tp", None), P())
    out_specs = P(("ctx", "tp"), None)
    return jax.shard_map(
        on_device, mesh=mesh, in_specs=in_specs, out_specs=out_specs, check_vma=False
    )
```

time: 24.1 us -> 21.6 us (0.90)
  the two profiles are of different devices: /device:TPU:16 before, /device:TPU:8 now
where the time goes in v3:
time: 21.6 us; the launch traced here: 21.5 us
  Pallas kernels  20.8 us (96%)
  local copies, waits for them, and re-layouts  0.68 us (3%)
    pallas_call x1, Pallas kernels, on_device(): pl.pallas_call(functools.partial(kernel, n, chunk), out_shape=jax.ShapeDt...  20.8 us
    unnamed x1, local copies, waits for them, and re-layouts  0.68 us

profile of v3, /device:TPU:8, one launch (start us, length us, event | category | flops | bytes accessed | tf_op | source)
XLA Modules:
  0.0 21.5 jit_solution(14544365591804869623)
XLA Ops:
  0.0 20.8 %shard_map.55 = bf16[32,3072]{1,0:T(8,128)(2,1)S(1)} custom-call(s32[16]{0:T(128)} %counts_ref.1, bf16[64,768]{1,0:T(8,128)(2,1)} %q_hbm.1, bf16[64,768]{1,0:T(8,128)(2,1)} %k_hbm.1, bf16[64,768]{1,0:T(8,128)(2,1)} %v_hbm.1, bf16[768,3072]{1,0:T(8,128)(2,1)} %wo_hbm.1), custom_call_target="tpu_custom_call" | custom-call | tf_op jit(solution)/shard_map/pallas_call | solution.py:691
  20.8 0.7 %copy.7 = bf16[32,3072]{1,0:T(8,128)(2,1)} copy(bf16[32,3072]{1,0:T(8,128)(2,1)S(1)} %shard_map.55) | data formatting | bytes 393216

commit v4 on v3

--- a/solution.py
+++ b/solution.py
@@ -23,19 +23,20 @@
 
 def host_places(size, head_count):
     top = size - LAYER
-    order = [top + i for i in (0, 2, 1, 3)] + list(range(top))
+    order = [top + i for i in (0, 2, 1, 3)] + [0, 2] + [i for i in range(top) if i not in (0, 2)]
     return order[:head_count]
 
 
 def kernel(
     n,
     chunk,
-    counts_ref,
+    counts_hbm,
     q_hbm,
     k_hbm,
     v_hbm,
     wo_hbm,
     out_ref,
+    counts_ref,
     q_ref,
     k_pal,
     v_pal,
@@ -53,6 +54,7 @@
     kept,
     outgoing,
     incoming,
+    counts_sem,
     in_sem,
     wo_sem,
     k_send,
@@ -115,6 +117,8 @@
     for b in range(2):
         pltpu.make_async_copy(q_hbm.at[pl.ds(start_of(b), half), :], q_ref.at[b], in_sem.at[2]).start()
 
+    counts_copy = pltpu.make_async_copy(counts_hbm, counts_ref, counts_sem)
+    counts_copy.start()
     wo_copy = pltpu.make_async_copy(wo_hbm, wo_all, wo_sem)
     first_pair = both(both(is_base, is_lower), lane < 2)
     pl.when(first_pair)(wo_copy.start)
@@ -199,6 +203,7 @@
         arrived(k_pal.at[lane], in_sem.at[0])
         arrived(v_pal.at[lane], in_sem.at[1])
         arrived(q_ref, in_sem.at[2])
+        counts_copy.wait()
 
     def to_hosts(give):
         for h in nearest_last:
@@ -217,27 +222,6 @@
             def _():
                 for h in nearest_last:
                     give_far(h, b).start()
-
-    @pl.when(both(is_base, lane == 0))
-    def _():
-        for kind in range(2):
-            pal(kind, 0, 1).start()
-
-    @pl.when(both(is_base, lane == 2))
-    def _():
-        for kind in range(2):
-            pal(kind, 2, 3).start()
-
-    to_far(0, is_upper)
-    to_far(1, is_base)
-    to_hosts(give_k)
-
-    @pl.when(both(is_upper, is_top))
-    def _():
-        to_hosts(give_q)
-
-    to_hosts(give_v)
-    to_far(1, is_top)
 
     @pl.when(is_host)
     def _():
@@ -249,6 +233,27 @@
             pltpu.make_async_copy(
                 q_ref.at[:, :, my_cols], q_in.at[NEAR, :, rows_of(local, half)], q_recv
             ).start()
+
+    @pl.when(both(is_base, lane == 0))
+    def _():
+        for kind in range(2):
+            pal(kind, 0, 1).start()
+
+    @pl.when(both(is_base, lane == 2))
+    def _():
+        for kind in range(2):
+            pal(kind, 2, 3).start()
+
+    to_far(0, is_upper)
+    to_far(1, is_base)
+    to_hosts(give_k)
+
+    @pl.when(both(is_upper, is_top))
+    def _():
+        to_hosts(give_q)
+
+    to_hosts(give_v)
+    to_far(1, is_top)
 
     @pl.when(both(is_lower, is_top))
     def _():
@@ -396,7 +401,7 @@
         top, acc = end(begun)
         first = t * far_frames
         acc_out[FAR, b, first * half : (first + far_frames) * half, :] = acc[:, :HEAD_DIM].astype(jnp.bfloat16)
-        frames = range(first + far_frames - 1, first - 1, -1)
+        frames = sorted(range(first, first + far_frames), key=lambda j: (j % LAYER >= LAYER // 2, -j))
         mine = [p for p, (at, rows) in enumerate(parts) if at // half == b]
         post(FAR, lambda j, dev: acc_copies(FAR, mine[0], j, dev), frames)
         stats_from(FAR, b, first, top, acc)
@@ -458,18 +463,29 @@
                 arrived(v_in, v_recv)
             serve_all_near(begun)
 
+        def wait_far(b):
+            with jax.named_scope("wf"):
+                arrived(q_in.at[FAR, b], far_recv.at[b])
+
         def host_both():
-            with jax.named_scope("wf"):
-                arrived(q_in.at[FAR, 0], far_recv.at[0])
-            with jax.named_scope("bf"):
-                begun = begin_far(0, 0) if size == far_frames and key_tiles == 1 else None
-            with jax.named_scope("wv"):
-                arrived(v_in, v_recv)
-            serve_all_far(0, begun)
-            wait_near()
-            serve_all_near(None)
-            with jax.named_scope("wf"):
-                arrived(q_in.at[FAR, 1], far_recv.at[1])
+            @pl.when(is_top)
+            def _():
+                wait_far(0)
+                with jax.named_scope("bf"):
+                    begun = begin_far(0, 0) if size == far_frames and key_tiles == 1 else None
+                with jax.named_scope("wv"):
+                    arrived(v_in, v_recv)
+                serve_all_far(0, begun)
+                wait_near()
+                serve_all_near(None)
+
+            @pl.when(is_base)
+            def _():
+                host_near()
+                wait_far(0)
+                serve_all_far(0, None)
+
+            wait_far(1)
             serve_all_far(1, None)
 
         if split:
@@ -573,19 +589,32 @@
                     else:
                         kept[:, c * chunk : (c + 1) * chunk] = part
 
-    @pl.when(is_base)
-    def _():
-        def pass_on(frame, to):
-            for kind in range(2):
-                arrived((k_pal, v_pal)[kind].at[frame], pal_recv.at[kind, frame])
-                if to is not None:
-                    pal(kind, frame, to).start()
-
+    def pass_on(frame, to):
+        for kind in range(2):
+            arrived((k_pal, v_pal)[kind].at[frame], pal_recv.at[kind, frame])
+            if to is not None:
+                pal(kind, frame, to).start()
+
+    @pl.when(both(is_base, lane < 2))
+    def _():
         with jax.named_scope("pal"):
 
             @pl.when(lane == 1)
             def _():
                 pass_on(0, None)
+
+        with jax.named_scope("lev"):
+            attend_level()
+
+        @pl.when(is_lower)
+        def _():
+            own_rows((0,), False, False)
+
+    pl.when(is_host)(host)
+
+    @pl.when(both(is_base, lane >= 2))
+    def _():
+        with jax.named_scope("pal"):
 
             @pl.when(lane == 2)
             def _():
@@ -604,8 +633,6 @@
         @pl.when(is_lower)
         def _():
             own_rows((0,), False, False)
-
-    pl.when(is_host)(host)
 
     @pl.when(both(is_base, is_lower))
     def _():
@@ -692,7 +719,7 @@
         functools.partial(kernel, n, chunk),
         out_shape=jax.ShapeDtypeStruct((half, width), jnp.bfloat16),
         in_specs=[
-            pl.BlockSpec(memory_space=pltpu.SMEM),
+            pl.BlockSpec(memory_space=pltpu.HBM),
             pl.BlockSpec(memory_space=pltpu.HBM),
             pl.BlockSpec(memory_space=pltpu.HBM),
             pl.BlockSpec(memory_space=pltpu.HBM),
@@ -700,6 +727,7 @@
         ],
         out_specs=pl.BlockSpec(memory_space=vmem),
         scratch_shapes=[
+            pltpu.SMEM((n,), jnp.int32),
             vmem((2, half, columns), jnp.bfloat16),
             vmem((LAYER, tok_rows, columns), jnp.bfloat16),
             vmem((LAYER, tok_rows, columns), jnp.bfloat16),
@@ -717,6 +745,7 @@
             vmem((half, width), jnp.float32),
             vmem((2, chunks, half // 2, chunk), jnp.bfloat16),
             vmem((2, chunks, half // 2, chunk), jnp.bfloat16),
+            dma,
             dma((3,)),
             dma,
             dma,

time: 21.6 us -> 20.9 us (0.968)
  the two profiles are of different devices: /device:TPU:8 before, /device:TPU:16 now
where the time goes in v4:
time: 20.9 us; the launch traced here: 20.6 us
  Pallas kernels  19.9 us (95%)
  local copies, waits for them, and re-layouts  0.68 us (3%)
    pallas_call x1, Pallas kernels, on_device(): pl.pallas_call(functools.partial(kernel, n, chunk), out_shape=jax.ShapeDt...  19.9 us
    unnamed x1, local copies, waits for them, and re-layouts  0.68 us

profile of v4, /device:TPU:16, one launch (start us, length us, event | category | flops | bytes accessed | tf_op | source)
XLA Modules:
  0.0 20.6 jit_solution(7096875751402188844)
XLA Ops:
  0.0 19.9 %shard_map.55 = bf16[32,3072]{1,0:T(8,128)(2,1)S(1)} custom-call(s32[16]{0:T(128)} %counts_hbm.1, bf16[64,768]{1,0:T(8,128)(2,1)} %q_hbm.1, bf16[64,768]{1,0:T(8,128)(2,1)} %k_hbm.1, bf16[64,768]{1,0:T(8,128)(2,1)} %v_hbm.1, bf16[768,3072]{1,0:T(8,128)(2,1)} %wo_hbm.1), custom_call_target="tpu_custom_call" | custom-call | tf_op jit(solution)/shard_map/pallas_call | solution.py:718
  19.9 0.7 %copy.7 = bf16[32,3072]{1,0:T(8,128)(2,1)} copy(bf16[32,3072]{1,0:T(8,128)(2,1)S(1)} %shard_map.55) | data formatting | bytes 393216
